TPU v7x, 512 devices: a whole 4x8x8 slice. The times are simulated.
512 devices in a mesh: dp: 4 (over z_lo, core), seq: 8 (over y), vocab: 16 (over z_hi, x).
Axes of the slice: x: 4, y: 8, z: 8 (z_hi: 4, z_lo: 2; z = z_hi * 2 + z_lo), core: 2. Of those that a mesh axis runs over, the one named last changes fastest.
Arguments:
- queries: bfloat16 [4, 256, 4096], P('dp', 'seq', 'vocab'), may hold values from -64 to 64
- enc_keys: bfloat16 [4, 1024, 4096], P('dp', 'seq', 'vocab'), may hold values from -6 to 6
- enc_values: bfloat16 [4, 1024, 4096], P('dp', 'seq', 'vocab'), may hold values from -6 to 6
- enc_lengths: int32 [4], P('dp'), may hold values from 256 to 1024, as said below
- out_proj: bfloat16 [4096, 4096], P('vocab', 'seq'), may hold values from -0.375 to 0.375
- residual: bfloat16 [4, 256, 4096], P('dp', None, 'seq'), may hold values from -270 to 270
- norm_gain: float32 [4096], P('seq'), may hold values from 0.4 to 1.6
- head_weight: bfloat16 [4096, 32128], P('seq', 'vocab'), may hold values from -1 to 1
- targets: int32 [4, 256], P('dp', 'seq'), may hold values from 0 to 32127
Outputs:
- mean_loss: float32 [], replicated
- head_grad: bfloat16 [4096, 32128], P('seq', 'vocab')
- key_grad: float32 [4, 1024, 4096], P('dp', 'seq', 'vocab')
- value_grad: float32 [4, 1024, 4096], P('dp', 'seq', 'vocab')
Inputs may be any that keep to these rules, and one draw needn't show every extreme that they name: `enc_lengths`: each example has at least 256 unpadded positions; some example has none padded.
All inputs are finite; a program needn't handle non-finite values.
Results may differ from a plain program's by a relative error of at most 0.02.
Values may be sent and summed in bfloat16 or wider, within the bound.
A program may use at most 64 MiB of HBM per device.

v0:
```python
import jax
import jax.numpy as jnp
from jax import lax
from jax.sharding import PartitionSpec as P

D = 4096
HDIM = 256
zloss_weight = 0.0001
norm_epsilon = 1e-06


def body(
    queries, enc_keys, enc_values, enc_lengths, out_proj, residual, norm_gain, head_weight, targets
):
    examples, tgt_rows, features = queries.shape
    heads_here = features // HDIM
    vocab_cols = head_weight.shape[1]
    all_targets = tgt_rows * lax.axis_size("seq")
    score_scale = HDIM ** (-0.5)
    key_all, value_all = (
        lax.all_gather(enc_keys, "seq", axis=1, tiled=True),
        lax.all_gather(enc_values, "seq", axis=1, tiled=True),
    )
    enc_rows = key_all.shape[1]
    query_heads = queries.reshape(examples, tgt_rows, heads_here, HDIM)
    key_heads = key_all.reshape(examples, enc_rows, heads_here, HDIM)
    value_heads = value_all.reshape(examples, enc_rows, heads_here, HDIM)
    scores = (
        jnp.einsum("bthd,bjhd->bhtj", query_heads, key_heads, preferred_element_type=jnp.float32)
        * score_scale
    )
    valid_keys = lax.broadcasted_iota(jnp.int32, (examples, enc_rows), 1) < enc_lengths[:, None]
    scores = jnp.where(valid_keys[:, None, None, :], scores, -jnp.inf)
    score_peak = jnp.max(scores, axis=-1, keepdims=True)
    score_exp = jnp.exp(scores - score_peak)
    weights_full = score_exp / jnp.sum(score_exp, axis=-1, keepdims=True)
    weights_half = weights_full.astype(jnp.bfloat16)
    attended = jnp.einsum(
        "bhtj,bjhd->tbhd", weights_half, value_heads, preferred_element_type=jnp.float32
    )
    attended = attended.astype(jnp.bfloat16).reshape(tgt_rows, examples, features)
    attended_all = lax.all_gather(attended, "seq", axis=0, tiled=True)
    mixed_part = jnp.einsum(
        "tbf,fd->tbd", attended_all, out_proj, preferred_element_type=jnp.float32
    )
    mixed_rows = lax.psum(mixed_part, "vocab") + jnp.swapaxes(residual, 0, 1).astype(jnp.float32)
    square_sum = lax.psum(jnp.sum(mixed_rows * mixed_rows, axis=-1), "seq")
    inverse_rms = lax.rsqrt(square_sum / D + norm_epsilon)
    normed = (mixed_rows * inverse_rms[..., None] * norm_gain).astype(jnp.bfloat16)
    row_block = normed
    logits = lax.psum_scatter(
        jnp.einsum("tbd,dv->tbv", row_block, head_weight, preferred_element_type=jnp.float32),
        "seq",
        scatter_dimension=0,
        tiled=True,
    )
    column_ids = (
        lax.broadcasted_iota(jnp.int32, (1, 1, vocab_cols), 2)
        + lax.axis_index("vocab") * vocab_cols
    )
    target_hit = column_ids == jnp.swapaxes(targets, 0, 1)[..., None]
    local_target = jnp.sum(jnp.where(target_hit, logits, 0.0), axis=-1)
    row_peak = lax.pmax(jnp.max(logits, axis=-1), "vocab")
    exp_total, target_logit = lax.psum(
        (jnp.sum(jnp.exp(logits - row_peak[..., None]), axis=-1), local_target), "vocab"
    )
    log_total = row_peak + jnp.log(exp_total)
    token_loss = log_total - target_logit + zloss_weight * log_total * log_total
    mean_loss = lax.psum(jnp.sum(token_loss), ("dp", "seq")) / (
        examples * lax.axis_size("dp") * all_targets
    )
    logit_grad = (
        jnp.exp(logits - log_total[..., None]) * (1.0 + 2.0 * zloss_weight * log_total)[..., None]
        - target_hit.astype(jnp.float32)
    ).astype(jnp.bfloat16)
    grad_piece = lax.all_gather(logit_grad, "seq", axis=0, tiled=True)
    row_block = normed
    weight_acc = jnp.einsum(
        "tbd,tbv->dv", row_block, grad_piece, preferred_element_type=jnp.float32
    )
    hidden_part = jnp.einsum(
        "tbv,dv->tbd", grad_piece, head_weight, preferred_element_type=jnp.float32
    )
    head_total = lax.psum(weight_acc.astype(jnp.bfloat16), "dp")
    summed_grad = lax.psum(hidden_part, "vocab")
    gated = summed_grad * norm_gain
    dot_row = lax.psum(jnp.sum(gated * mixed_rows, axis=-1), "seq")
    mixed_grad = (
        gated * inverse_rms[..., None] - mixed_rows * (inverse_rms**3 * dot_row / D)[..., None]
    ).astype(jnp.bfloat16)
    row_block = mixed_grad
    attended_grad = lax.psum_scatter(
        jnp.einsum("tbd,fd->tbf", row_block, out_proj, preferred_element_type=jnp.float32),
        "seq",
        scatter_dimension=0,
        tiled=True,
    ).astype(jnp.bfloat16)
    grad_heads = attended_grad.reshape(tgt_rows, examples, heads_here, HDIM)
    prob_grad = jnp.einsum(
        "tbhd,bjhd->bhtj", grad_heads, value_heads, preferred_element_type=jnp.float32
    )
    score_grad = weights_full * (
        prob_grad - jnp.sum(weights_full * prob_grad, axis=-1, keepdims=True)
    )
    score_half = (score_grad * score_scale).astype(jnp.bfloat16)
    value_part = jnp.einsum(
        "bhtj,tbhd->bjhd", weights_half, grad_heads, preferred_element_type=jnp.float32
    )
    key_part = jnp.einsum(
        "bhtj,bthd->bjhd", score_half, query_heads, preferred_element_type=jnp.float32
    )
    key_grad, value_grad = (
        lax.psum_scatter(
            key_part.reshape(examples, enc_rows, features).astype(jnp.bfloat16),
            "seq",
            scatter_dimension=1,
            tiled=True,
        ).astype(jnp.float32),
        lax.psum_scatter(
            value_part.reshape(examples, enc_rows, features).astype(jnp.bfloat16),
            "seq",
            scatter_dimension=1,
            tiled=True,
        ).astype(jnp.float32),
    )
    return (mean_loss, head_total, key_grad, value_grad)


def solution(mesh):
    placed = (
        P("dp", "seq", "vocab"),
        P("dp", "seq", "vocab"),
        P("dp", "seq", "vocab"),
        P("dp"),
        P("vocab", "seq"),
        P("dp", None, "seq"),
        P("seq"),
        P("seq", "vocab"),
        P("dp", "seq"),
    )
    return jax.shard_map(
        body,
        mesh=mesh,
        in_specs=placed,
        out_specs=(P(), P("seq", "vocab"), P("dp", "seq", "vocab"), P("dp", "seq", "vocab")),
        check_vma=False,
    )
```

profile of v0, /device:TPU:1, one launch (start us, length us, event | category | flops | bytes accessed | tf_op | source)
XLA Modules:
  0.0 880.7 jit_solution(10574764354764928775)
XLA Ops:
  7.2 0.0 copy-start
  7.2 0.0 copy-start.5
  7.2 0.0 all-reduce.7.cloned.1.call-start
  7.2 22.1 %all_gather.12 = bf16[1,1024,256]{2,1,0:T(8,128)(2,1)S(1)} all-gather(bf16[1,128,256]{2,1,0:T(8,128)(2,1)} %param.10), channel_id=1, replica_groups=mesh['dp'=4,'seq'=8,'vocab'=16] {'seq'}, dimensions={1}, use_global_device_ids=true | all-gather | bytes 589824 | tf_op jit(solution)/shard_map/all_gather | solution.py:21
  30.0 19.8 %all_gather.13 = bf16[1,1024,256]{2,1,0:T(8,128)(2,1)S(1)} all-gather(bf16[1,128,256]{2,1,0:T(8,128)(2,1)} %param.11), channel_id=1, replica_groups=mesh['dp'=4,'seq'=8,'vocab'=16] {'seq'}, dimensions={1}, use_global_device_ids=true | all-gather | bytes 589824 | tf_op jit(solution)/shard_map/all_gather | solution.py:22
  49.8 1.1 fusion.42
  51.0 0.2 fusion.21
  51.2 0.0 copy-done.6
  51.2 0.2 fusion.3
  51.5 18.9 %all-gather = bf16[256,1,1,256]{3,0,2,1:T(8,128)(2,1)S(1)} all-gather(bf16[32,1,1,256]{3,0,2,1:T(8,128)(2,1)S(1)} %fusion.3), channel_id=2, replica_groups=mesh['dp'=4,'seq'=8,'vocab'=16] {'seq'}, dimensions={0}, use_global_device_ids=true | all-gather | bytes 147456 | tf_op jit(solution)/shard_map/all_gather | solution.py:42
  70.4 1.0 convolution_bitcast_fusion.2
  71.4 0.0 all-reduce.7.cloned.1.call-update
  71.4 0.0 all-reduce.13.cloned.1.call-start
  71.5 182.3 %all-reduce.7.cloned.1.call-done = f32[256,1,512]{2,0,1:T(8,128)} async-done(((f32[256,1,512]{2,0,1:T(8,128)}), f32[256,1,512]{2,0,1:T(8,128)}) %all-reduce.7.cloned.1.call-update) | async-done | bytes 524304 | tf_op jit(solution)/shard_map/psum | solution.py:46
  253.8 1.2 multiply_reduce_fusion.1
  255.0 13.7 %psum.57 = f32[256,1]{0,1:T(1,128)S(1)} all-reduce(f32[256,1]{0,1:T(1,128)S(1)} %bitcast.113), channel_id=1, replica_groups=mesh['dp'=4,'seq'=8,'vocab'=16] {'seq'}, use_global_device_ids=true, to_apply=%region_4.5 | all-reduce | flops 256 | bytes 2048 | tf_op jit(solution)/shard_map/psum | solution.py:47
  268.7 0.0 copy-done.9
  268.7 1.2 fusion.13
  269.9 2.0 convolution_bitcast_fusion
  271.9 6.1 copy.18
  278.0 0.0 all-reduce.13.cloned.1.call-update
  278.1 0.0 all-reduce.11.cloned.1.call-start
  278.1 1.3 dynamic-slice
  280.1 92.1 %all-reduce.13.cloned.1.call-done = f32[256,1,2008]{2,1,0:T(1,128)} async-done(((f32[256,1,2008]{2,1,0:T(1,128)}), f32[256,1,2008]{2,1,0:T(1,128)}) %all-reduce.13.cloned.1.call-update) | async-done | bytes 2056208
  372.2 1.3 fusion.41
  373.6 38.9 %pmax.7 = f32[32,1]{0,1:T(1,128)S(1)} all-reduce(f32[32,1]{0,1:T(1,128)S(1)} %bitcast.120), channel_id=1, replica_groups=mesh['dp'=4,'seq'=8,'vocab'=16] {'vocab'}, use_global_device_ids=true, to_apply=%region_7.8 | all-reduce | flops 32 | bytes 256 | tf_op jit(solution)/shard_map/pmax | solution.py:63
  412.5 0.6 exponential_reduce_fusion
  413.0 0.2 fusion.10
  413.2 32.1 %all-reduce.1 = (f32[32,1]{0,1:T(1,128)S(1)}, f32[32,1]{0,1:T(1,128)S(1)}) all-reduce(f32[32,1]{0,1:T(1,128)S(1)} %bitcast.118, f32[32,1]{0,1:T(1,128)S(1)} %bitcast.119), channel_id=1, replica_groups=mesh['dp'=4,'seq'=8,'vocab'=16] {'vocab'}, use_global_device_ids=true, to_apply=%region_9.10 | all-reduce | flops 64 | bytes 512 | tf_op jit(solution)/shard_map/psum | solution.py:64
  445.3 0.6 fusion.37
  446.0 0.2 fusion.12
  446.1 20.6 %all_gather.15 = bf16[256,1,2008]{2,0,1:T(8,128)(2,1)S(1)} all-gather(bf16[32,1,2008]{2,0,1:T(8,128)(2,1)S(1)} %fusion.12), channel_id=1, replica_groups=mesh['dp'=4,'seq'=8,'vocab'=16] {'seq'}, dimensions={0}, use_global_device_ids=true | all-gather | bytes 1156608 | tf_op jit(solution)/shard_map/all_gather | solution.py:76
  466.7 1.0 copy-done.2
  467.7 1.5 convolution_bitcast_fusion.1
  469.2 0.0 all-reduce.11.cloned.1.call-update
  469.3 0.0 reduce-scatter.6.cloned.1.call-start
  469.3 178.2 %all-reduce.11.cloned.1.call-done = f32[256,1,512]{2,0,1:T(8,128)} async-done(((f32[256,1,512]{2,0,1:T(8,128)}), f32[256,1,512]{2,0,1:T(8,128)}) %all-reduce.11.cloned.1.call-update) | async-done | bytes 524304 | tf_op jit(solution)/shard_map/psum | solution.py:85
  647.5 1.2 multiply_reduce_fusion
  648.8 13.7 %psum.63 = f32[256,1]{0,1:T(1,128)S(1)} all-reduce(f32[256,1]{0,1:T(1,128)S(1)} %bitcast.114), channel_id=1, replica_groups=mesh['dp'=4,'seq'=8,'vocab'=16] {'seq'}, use_global_device_ids=true, to_apply=%region_17.18 | all-reduce | flops 256 | bytes 2048 | tf_op jit(solution)/shard_map/psum | solution.py:87
  662.5 2.1 convolution_bitcast_fusion.3
  664.5 0.0 reduce-scatter.6.cloned.1.call-update
  664.5 0.0 reduce-scatter.10.cloned.1.call-start
  664.6 43.5 %reduce-scatter.6.cloned.1.call-done = f32[32,1,256]{2,0,1:T(8,128)} async-done(((f32[256,1,256]{2,0,1:T(8,128)}), f32[32,1,256]{2,0,1:T(8,128)}) %reduce-scatter.6.cloned.1.call-update) | async-done | bytes 32784 | tf_op jit(solution)/shard_map/reduce_scatter | solution.py:92
  708.1 1.2 fusion.1
  709.3 0.0 copy-start.7
  709.3 2.0 copy.22
  711.3 2.2 copy.28
  713.5 0.0 reduce-scatter.10.cloned.1.call-update
  713.5 0.0 reduce-scatter.8.cloned.1.call-start
  713.6 1.4 multiply_reduce_fusion.2
  715.0 1.2 fusion
  716.2 0.0 reduce-scatter.8.cloned.1.call-update
  716.2 0.0 all-reduce.9.cloned.1.call-start
  716.3 2.0 convolution_convert_fusion
  718.4 0.0 all-reduce.9.cloned.1.call-update
  718.4 60.4 %psum.60 = f32[]{:T(128)} all-reduce(f32[]{:T(128)} %get-tuple-element.26), channel_id=1, replica_groups=mesh['dp'=4,'seq'=8,'vocab'=16] {'dp','seq'}, use_global_device_ids=true, to_apply=%region_13.14 | all-reduce | flops 1 | bytes 8 | tf_op jit(solution)/shard_map/psum | solution.py:69
  779.4 0.0 reduce-scatter.10.cloned.1.call-done
  779.4 0.9 reshape_bitcast_fusion
  780.4 0.1 copy.23
  780.5 0.8 copy.21
  781.3 13.0 %reduce-scatter.8.cloned.1.call-done = bf16[1,128,256]{2,1,0:T(8,128)(2,1)} async-done(((bf16[1,1024,256]{2,1,0:T(8,128)(2,1)}), bf16[1,128,256]{2,1,0:T(8,128)(2,1)}) %reduce-scatter.8.cloned.1.call-update) | async-done | bytes 65552 | tf_op jit(solution)/shard_map/reduce_scatter | solution.py:113
  794.3 1.5 convert_element_type.128
  795.8 74.0 %all-reduce.9.cloned.1.call-done = bf16[512,2008]{0,1:T(8,128)(2,1)} async-done(((bf16[512,2008]{0,1:T(8,128)(2,1)}), bf16[512,2008]{0,1:T(8,128)(2,1)}) %all-reduce.9.cloned.1.call-update) | async-done | bytes 2056208 | tf_op jit(solution)/shard_map/psum | solution.py:84
  869.7 3.0 copy.34
  (20 shorter events, 0.1 us)
Async XLA Ops:
  7.2 262.7 %copy-start = (bf16[512,2008]{0,1:T(8,128)(2,1)S(1)}, bf16[512,2008]{0,1:T(8,128)(2,1)}, u32[]{:S(2)}) copy-start(bf16[512,2008]{0,1:T(8,128)(2,1)} %param.16) | copy-start | bytes 6168580
  7.2 63.2 %copy-start.5 = (bf16[256,512]{1,0:T(8,128)(2,1)S(1)}, bf16[256,512]{1,0:T(8,128)(2,1)}, u32[]{:S(2)}) copy-start(bf16[256,512]{1,0:T(8,128)(2,1)} %param.13) | copy-start | bytes 786436
  7.2 246.6 %all-reduce.7.cloned.1.call-start = ((), (), s32[]{:S(2)}) async-start(), calls=%async_computation.3 | async-start | bytes 1048576 | tf_op jit(solution)/shard_map/psum | solution.py:46
  29.3 224.5 %copy-start.4 = (bf16[1,256,512]{2,1,0:T(8,128)(2,1)S(1)}, bf16[1,256,512]{2,1,0:T(8,128)(2,1)}, u32[]{:S(2)}) copy-start(bf16[1,256,512]{2,1,0:T(8,128)(2,1)} %param.14) | copy-start | bytes 786436
  49.8 1.4 copy-start.6
  49.8 218.9 %copy-start.9 = (f32[512]{0:T(512)S(1)}, f32[512]{0:T(512)}, u32[]{:S(2)}) copy-start(f32[512]{0:T(512)} %param.15) | copy-start | bytes 6148
  71.4 300.8 %all-reduce.13.cloned.1.call-start = ((), (), s32[]{:S(2)}) async-start(), calls=%async_computation.9 | async-start | bytes 4194304
  278.0 135.0 %copy-start.10 = (s32[1,32]{1,0:T(1,128)S(1)}, s32[1,32]{1,0:T(1,128)}, u32[]{:S(2)}) copy-start(s32[1,32]{1,0:T(1,128)} %param.17) | copy-start | bytes 388
  278.1 369.5 %all-reduce.11.cloned.1.call-start = ((), (), s32[]{:S(2)}) async-start(), calls=%async_computation.5 | async-start | bytes 1048576 | tf_op jit(solution)/shard_map/psum | solution.py:85
  466.7 1.0 copy-start.2
  467.7 179.8 %copy-start.1 = (f32[256,1,512]{2,0,1:T(8,128)S(1)}, f32[256,1,512]{2,0,1:T(8,128)}, u32[]{:S(2)}) copy-start(f32[256,1,512]{2,0,1:T(8,128)} %all-reduce.7.cloned.1.call-done) | copy-start | bytes 1572868
  469.3 238.8 %reduce-scatter.6.cloned.1.call-start = ((), (), s32[]{:S(2)}) async-start(), calls=%async_computation.6 | async-start | bytes 294912 | tf_op jit(solution)/shard_map/reduce_scatter | solution.py:92
  664.5 114.9 %reduce-scatter.10.cloned.1.call-start = ((), (), s32[]{:S(2)}) async-start(), calls=%async_computation.8 | async-start | bytes 589824
  708.1 5.5 copy-start.8
  709.3 5.7 copy-start.7
  711.3 5.0 copy-start.3
  713.5 80.8 %reduce-scatter.8.cloned.1.call-start = ((), (), s32[]{:S(2)}) async-start(), calls=%async_computation.7 | async-start | bytes 589824 | tf_op jit(solution)/shard_map/reduce_scatter | solution.py:113
  716.2 153.5 %all-reduce.9.cloned.1.call-start = ((), (), s32[]{:S(2)}) async-start(), calls=%async_computation.4 | async-start | bytes 4112384 | tf_op jit(solution)/shard_map/psum | solution.py:84
Sparse Core Ops, SparseCore 0:
  71.6 182.1 all-reduce.6
  278.2 93.9 all-reduce.12
  469.4 178.1 all-reduce.10
  664.7 43.3 reduce-scatter.5
  713.6 39.4 reduce-scatter.9
  755.8 38.4 reduce-scatter.7
  798.1 71.5 all-reduce.8
where the time goes:
time: 882 us; the launch traced here: 881 us
  waiting for transfers between devices  583 us (66%)
  blocking collectives  240 us (27%)
  local copies, waits for them, and re-layouts  17.4 us (2%)
  between operations  17.4 us (2%)
  matrix products  13.9 us (2%)
    psum x1, waiting for transfers between devices, body(): lax.psum(mixed_part, 'vocab')  182 us
    psum x1, waiting for transfers between devices, body(): summed_grad = lax.psum(hidden_part, 'vocab')  178 us
    unnamed x9, waiting for transfers between devices  92.3 us
    psum x1, waiting for transfers between devices, body(): head_total = lax.psum(weight_acc.astype(jnp.bfloat16), 'dp')  74 us
    psum x1, blocking collectives, body(): lax.psum(jnp.sum(token_loss), ('dp', 'seq'))  60.4 us
    reduce_scatter x1, waiting for transfers between devices, body(): lax.psum_scatter(jnp.einsum('tbd,fd->tbf', row_block, out_proj, preferred...  43.5 us
    pmax x1, blocking collectives, body(): row_peak = lax.pmax(jnp.max(logits, axis=-1), 'vocab')  38.9 us
    psum x1, blocking collectives, body(): lax.psum((jnp.sum(jnp.exp(logits - row_peak[..., None]), axis=-1), local_...  32.1 us
  transfers between devices with their start and end apart: 7, of which 6 were waited for; matrix products, arithmetic and copies ran while one was open for 1% of the time, Pallas kernels for 0%

commit v1 on v0

--- a/solution.py
+++ b/solution.py
@@ -82,7 +82,7 @@
         "tbv,dv->tbd", grad_piece, head_weight, preferred_element_type=jnp.float32
     )
     head_total = lax.psum(weight_acc.astype(jnp.bfloat16), "dp")
-    summed_grad = lax.psum(hidden_part, "vocab")
+    summed_grad = jnp.sum(lax.all_gather(hidden_part, "vocab"), axis=0)
     gated = summed_grad * norm_gain
     dot_row = lax.psum(jnp.sum(gated * mixed_rows, axis=-1), "seq")
     mixed_grad = (

time: 882 us -> 837 us (0.949)
  waiting for transfers between devices: 583 us -> 535 us
    psum x1 -> x0, waiting for transfers between devices: 178 us -> none  [body(): summed_grad = lax.psum(hidden_part, 'vocab')]
    all_gather x0 -> x1, waiting for transfers between devices: none -> 140 us  [body(): summed_grad = jnp.sum(lax.all_gather(hidden_part, 'vocab'), axis=0)]
    reduce_scatter x1, waiting for transfers between devices: 43.5 us -> 32.8 us  [body(): lax.psum_scatter(jnp.einsum('tbd,fd->tbf', row_block, out_proj, preferred...]
where the time goes in v1:
time: 837 us; the launch traced here: 836 us
  waiting for transfers between devices  535 us (64%)
  blocking collectives  240 us (29%)
  local copies, waits for them, and re-layouts  18.1 us (2%)
  between operations  17.5 us (2%)
  matrix products  13.7 us (2%)
  other arithmetic  11.6 us (1%)
    psum x1, waiting for transfers between devices, body(): lax.psum(mixed_part, 'vocab')  182 us
    all_gather x1, waiting for transfers between devices, body(): summed_grad = jnp.sum(lax.all_gather(hidden_part, 'vocab'), axis=0)  140 us
    unnamed x9, waiting for transfers between devices  92.4 us
    psum x1, waiting for transfers between devices, body(): head_total = lax.psum(weight_acc.astype(jnp.bfloat16), 'dp')  73.7 us
    psum x1, blocking collectives, body(): lax.psum(jnp.sum(token_loss), ('dp', 'seq'))  60.4 us
    pmax x1, blocking collectives, body(): row_peak = lax.pmax(jnp.max(logits, axis=-1), 'vocab')  38.9 us
    reduce_scatter x1, waiting for transfers between devices, body(): lax.psum_scatter(jnp.einsum('tbd,fd->tbf', row_block, out_proj, preferred...  32.8 us
    psum x1, blocking collectives, body(): lax.psum((jnp.sum(jnp.exp(logits - row_peak[..., None]), axis=-1), local_...  32.1 us
  transfers between devices with their start and end apart: 7, of which 6 were waited for; matrix products, arithmetic and copies ran while one was open for 1% of the time, Pallas kernels for 0%

profile of v1, /device:TPU:1, one launch (start us, length us, event | category | flops | bytes accessed | tf_op | source)
XLA Modules:
  0.0 835.8 jit_solution(4153836605540388626)
XLA Ops:
  7.2 0.0 copy-start
  7.2 0.0 copy-start.7
  7.2 0.0 all-reduce.6.cloned.1.call-start
  8.1 21.9 %all_gather.19 = bf16[1,1024,256]{2,1,0:T(8,128)(2,1)S(1)} all-gather(bf16[1,128,256]{2,1,0:T(8,128)(2,1)} %param.11), channel_id=1, replica_groups=mesh['dp'=4,'seq'=8,'vocab'=16] {'seq'}, dimensions={1}, use_global_device_ids=true | all-gather | bytes 589824 | tf_op jit(solution)/shard_map/all_gather | solution.py:22
  30.0 20.0 %all_gather.18 = bf16[1,1024,256]{2,1,0:T(8,128)(2,1)S(1)} all-gather(bf16[1,128,256]{2,1,0:T(8,128)(2,1)} %param.10), channel_id=1, replica_groups=mesh['dp'=4,'seq'=8,'vocab'=16] {'seq'}, dimensions={1}, use_global_device_ids=true | all-gather | bytes 589824 | tf_op jit(solution)/shard_map/all_gather | solution.py:21
  50.1 1.1 fusion.43
  51.2 0.2 fusion.22
  51.4 0.2 fusion.3
  51.6 18.9 %all-gather = bf16[256,1,1,256]{3,0,2,1:T(8,128)(2,1)S(1)} all-gather(bf16[32,1,1,256]{3,0,2,1:T(8,128)(2,1)S(1)} %fusion.3), channel_id=2, replica_groups=mesh['dp'=4,'seq'=8,'vocab'=16] {'seq'}, dimensions={0}, use_global_device_ids=true | all-gather | bytes 147456 | tf_op jit(solution)/shard_map/all_gather | solution.py:42
  70.5 1.0 convolution_bitcast_fusion.1
  71.5 0.0 all-reduce.6.cloned.1.call-update
  71.6 0.0 all-reduce.10.cloned.1.call-start
  71.6 182.3 %all-reduce.6.cloned.1.call-done = f32[256,1,512]{2,0,1:T(8,128)} async-done(((f32[256,1,512]{2,0,1:T(8,128)}), f32[256,1,512]{2,0,1:T(8,128)}) %all-reduce.6.cloned.1.call-update) | async-done | bytes 524304 | tf_op jit(solution)/shard_map/psum | solution.py:46
  253.9 1.2 multiply_reduce_fusion.1
  255.1 13.7 %psum.50 = f32[256,1]{0,1:T(1,128)S(1)} all-reduce(f32[256,1]{0,1:T(1,128)S(1)} %bitcast.122), channel_id=1, replica_groups=mesh['dp'=4,'seq'=8,'vocab'=16] {'seq'}, use_global_device_ids=true, to_apply=%region_4.5 | all-reduce | flops 256 | bytes 2048 | tf_op jit(solution)/shard_map/psum | solution.py:47
  268.8 1.2 fusion.14
  270.0 0.7 copy-done.5
  270.7 2.0 convolution_bitcast_fusion
  272.7 6.1 copy.18
  278.8 0.0 all-reduce.10.cloned.1.call-update
  278.9 0.0 all-gather.4.cloned.1.call-start
  278.9 1.3 dynamic-slice
  280.9 92.3 %all-reduce.10.cloned.1.call-done = f32[256,1,2008]{2,1,0:T(1,128)} async-done(((f32[256,1,2008]{2,1,0:T(1,128)}), f32[256,1,2008]{2,1,0:T(1,128)}) %all-reduce.10.cloned.1.call-update) | async-done | bytes 2056208
  373.1 1.3 fusion.42
  374.5 38.9 %pmax.7 = f32[32,1]{0,1:T(1,128)S(1)} all-reduce(f32[32,1]{0,1:T(1,128)S(1)} %bitcast.129), channel_id=1, replica_groups=mesh['dp'=4,'seq'=8,'vocab'=16] {'vocab'}, use_global_device_ids=true, to_apply=%region_7.8 | all-reduce | flops 32 | bytes 256 | tf_op jit(solution)/shard_map/pmax | solution.py:63
  413.4 0.6 exponential_reduce_fusion
  413.9 0.2 fusion.11
  414.2 32.1 %all-reduce.1 = (f32[32,1]{0,1:T(1,128)S(1)}, f32[32,1]{0,1:T(1,128)S(1)}) all-reduce(f32[32,1]{0,1:T(1,128)S(1)} %bitcast.127, f32[32,1]{0,1:T(1,128)S(1)} %bitcast.128), channel_id=1, replica_groups=mesh['dp'=4,'seq'=8,'vocab'=16] {'vocab'}, use_global_device_ids=true, to_apply=%region_9.10 | all-reduce | flops 64 | bytes 512 | tf_op jit(solution)/shard_map/psum | solution.py:64
  446.3 0.6 fusion.38
  446.9 0.2 fusion.13
  447.0 20.6 %all_gather.21 = bf16[256,1,2008]{2,0,1:T(8,128)(2,1)S(1)} all-gather(bf16[32,1,2008]{2,0,1:T(8,128)(2,1)S(1)} %fusion.13), channel_id=1, replica_groups=mesh['dp'=4,'seq'=8,'vocab'=16] {'seq'}, dimensions={0}, use_global_device_ids=true | all-gather | bytes 1156608 | tf_op jit(solution)/shard_map/all_gather | solution.py:76
  467.6 1.0 copy-done.2
  468.6 1.5 fusion.4
  470.1 0.0 all-gather.4.cloned.1.call-update
  470.1 0.0 reduce-scatter.6.cloned.1.call-start
  470.2 140.3 %all-gather.4.cloned.1.call-done = f32[4096,512]{1,0:T(8,128)} async-done(((f32[256,512]{1,0:T(8,128)}), f32[4096,512]{1,0:T(8,128)}) %all-gather.4.cloned.1.call-update) | async-done | bytes 8388624 | tf_op jit(solution)/shard_map/all_gather | solution.py:85
  610.5 4.5 reduce.12
  614.9 0.2 multiply_reduce_fusion
  615.1 13.3 %psum.55 = f32[256,1]{0,1:T(1,128)S(1)} all-reduce(f32[256,1]{0,1:T(1,128)S(1)} %bitcast.123), channel_id=1, replica_groups=mesh['dp'=4,'seq'=8,'vocab'=16] {'seq'}, use_global_device_ids=true, to_apply=%region_17.18 | all-reduce | flops 256 | bytes 2048 | tf_op jit(solution)/shard_map/psum | solution.py:87
  628.4 2.0 convolution_bitcast_fusion.2
  630.3 0.0 reduce-scatter.6.cloned.1.call-update
  630.4 0.0 reduce-scatter.10.cloned.1.call-start
  630.4 32.8 %reduce-scatter.6.cloned.1.call-done = f32[32,1,256]{2,0,1:T(8,128)} async-done(((f32[256,1,256]{2,0,1:T(8,128)}), f32[32,1,256]{2,0,1:T(8,128)}) %reduce-scatter.6.cloned.1.call-update) | async-done | bytes 32784 | tf_op jit(solution)/shard_map/reduce_scatter | solution.py:92
  663.2 1.2 fusion.1
  664.4 0.0 copy-start.9
  664.4 2.0 copy.22
  666.4 2.2 copy.28
  668.6 0.0 reduce-scatter.10.cloned.1.call-update
  668.7 0.0 reduce-scatter.8.cloned.1.call-start
  668.7 1.4 multiply_reduce_fusion.2
  670.2 1.2 fusion
  671.4 0.0 reduce-scatter.8.cloned.1.call-update
  671.4 0.0 all-reduce.8.cloned.1.call-start
  671.5 2.0 convolution_convert_fusion
  673.5 0.0 all-reduce.8.cloned.1.call-update
  673.5 60.4 %psum.53 = f32[]{:T(128)} all-reduce(f32[]{:T(128)} %get-tuple-element.26), channel_id=1, replica_groups=mesh['dp'=4,'seq'=8,'vocab'=16] {'dp','seq'}, use_global_device_ids=true, to_apply=%region_13.14 | all-reduce | flops 1 | bytes 8 | tf_op jit(solution)/shard_map/psum | solution.py:69
  734.6 0.0 reduce-scatter.10.cloned.1.call-done
  734.6 0.9 reshape_bitcast_fusion
  735.5 0.1 copy.23
  735.7 0.8 copy.21
  736.5 13.2 %reduce-scatter.8.cloned.1.call-done = bf16[1,128,256]{2,1,0:T(8,128)(2,1)} async-done(((bf16[1,1024,256]{2,1,0:T(8,128)(2,1)}), bf16[1,128,256]{2,1,0:T(8,128)(2,1)}) %reduce-scatter.8.cloned.1.call-update) | async-done | bytes 65552 | tf_op jit(solution)/shard_map/reduce_scatter | solution.py:113
  749.7 1.5 convert_element_type.128
  751.2 73.7 %all-reduce.8.cloned.1.call-done = bf16[512,2008]{0,1:T(8,128)(2,1)} async-done(((bf16[512,2008]{0,1:T(8,128)(2,1)}), bf16[512,2008]{0,1:T(8,128)(2,1)}) %all-reduce.8.cloned.1.call-update) | async-done | bytes 2056208 | tf_op jit(solution)/shard_map/psum | solution.py:84
  824.8 3.0 copy.33
  (25 shorter events, 0.1 us)
Async XLA Ops:
  7.2 263.5 %copy-start = (bf16[512,2008]{0,1:T(8,128)(2,1)S(1)}, bf16[512,2008]{0,1:T(8,128)(2,1)}, u32[]{:S(2)}) copy-start(bf16[512,2008]{0,1:T(8,128)(2,1)} %param.16) | copy-start | bytes 6168580
  7.2 63.3 %copy-start.7 = (bf16[256,512]{1,0:T(8,128)(2,1)S(1)}, bf16[256,512]{1,0:T(8,128)(2,1)}, u32[]{:S(2)}) copy-start(bf16[256,512]{1,0:T(8,128)(2,1)} %param.13) | copy-start | bytes 786436
  7.2 246.7 %all-reduce.6.cloned.1.call-start = ((), (), s32[]{:S(2)}) async-start(), calls=%async_computation.3 | async-start | bytes 1048576 | tf_op jit(solution)/shard_map/psum | solution.py:46
  30.0 21.4 %copy-start.8 = (bf16[1,1024,256]{2,1,0:T(8,128)(2,1)}, bf16[1,1024,256]{2,1,0:T(8,128)(2,1)S(1)}, u32[]{:S(2)}) copy-start(bf16[1,1024,256]{2,1,0:T(8,128)(2,1)S(1)} %all_gather.19) | copy-start | bytes 1572868
  30.0 223.9 %copy-start.4 = (bf16[1,256,512]{2,1,0:T(8,128)(2,1)S(1)}, bf16[1,256,512]{2,1,0:T(8,128)(2,1)}, u32[]{:S(2)}) copy-start(bf16[1,256,512]{2,1,0:T(8,128)(2,1)} %param.14) | copy-start | bytes 786436
  50.1 218.8 %copy-start.11 = (f32[512]{0:T(512)S(1)}, f32[512]{0:T(512)}, u32[]{:S(2)}) copy-start(f32[512]{0:T(512)} %param.15) | copy-start | bytes 6148
  71.6 301.5 %all-reduce.10.cloned.1.call-start = ((), (), s32[]{:S(2)}) async-start(), calls=%async_computation.9 | async-start | bytes 4194304
  270.0 0.7 copy-start.5
  278.8 135.1 %copy-start.12 = (s32[1,32]{1,0:T(1,128)S(1)}, s32[1,32]{1,0:T(1,128)}, u32[]{:S(2)}) copy-start(s32[1,32]{1,0:T(1,128)} %param.17) | copy-start | bytes 388
  278.9 331.6 %all-gather.4.cloned.1.call-start = ((), (), s32[]{:S(2)}) async-start(), calls=%async_computation.7 | async-start | bytes 8912896 | tf_op jit(solution)/shard_map/all_gather | solution.py:85
  467.6 1.0 copy-start.2
  470.1 193.1 %reduce-scatter.6.cloned.1.call-start = ((), (), s32[]{:S(2)}) async-start(), calls=%async_computation.5 | async-start | bytes 294912 | tf_op jit(solution)/shard_map/reduce_scatter | solution.py:92
  610.5 4.5 copy-start.1
  630.4 104.2 %reduce-scatter.10.cloned.1.call-start = ((), (), s32[]{:S(2)}) async-start(), calls=%async_computation.8 | async-start | bytes 589824
  663.2 5.5 copy-start.10
  664.4 5.7 copy-start.9
  666.4 5.0 copy-start.3
  666.4 5.0 copy-start.6
  668.7 81.0 %reduce-scatter.8.cloned.1.call-start = ((), (), s32[]{:S(2)}) async-start(), calls=%async_computation.6 | async-start | bytes 589824 | tf_op jit(solution)/shard_map/reduce_scatter | solution.py:113
  671.4 153.4 %all-reduce.8.cloned.1.call-start = ((), (), s32[]{:S(2)}) async-start(), calls=%async_computation.4 | async-start | bytes 4112384 | tf_op jit(solution)/shard_map/psum | solution.py:84
Sparse Core Ops, SparseCore 0:
  71.7 182.1 all-reduce.5
  279.0 94.0 all-reduce.9
  470.3 140.1 all-gather.3
  630.5 32.7 reduce-scatter.5
  668.8 39.3 reduce-scatter.9
  711.1 38.5 reduce-scatter.7
  753.2 71.5 all-reduce.7
